TPU v7x, 32 devices: a whole 2x2x4 slice. The times are simulated.
32 devices in a mesh: dp: 8 (over y, x, core), mp: 4 (over z).
Axes of the slice: x: 2, y: 2, z: 4, core: 2. Of those that a mesh axis runs over, the one named last changes fastest.
Arguments:
- activations: bfloat16 [128, 288, 768], P(('dp', 'mp')), may hold values from -2.5 to 2.5
- cotangent: bfloat16 [128, 288, 768], P(('dp', 'mp')), may hold values from -2.5 to 2.5
- segments: int32 [128, 288], P('dp'), may hold values from 0 to 2, never falling along the last dimension, each value on 1 to 160 neighbouring positions
- triple_weight: bfloat16 [3, 768, 768], P(None, None, 'mp'), may hold values from -0.21875 to 0.21875
- query_value_bias: bfloat16 [2, 12, 64], P(None, 'mp'), may hold values from -1.5 to 1.5
- output_weight: bfloat16 [768, 768], P('mp'), may hold values from -0.875 to 0.875
- expand_weight: bfloat16 [768, 3072], P(None, 'mp'), may hold values from -0.21875 to 0.21875
- expand_bias: bfloat16 [48, 64], P('mp'), may hold values from -1.5 to 1.5
- shrink_weight: bfloat16 [3072, 768], P('mp'), may hold values from -0.109375 to 0.109375
- vector_params: bfloat16 [6, 768], replicated
- triple_master: float32 [3, 768, 768], P(None, 'dp', 'mp'), may hold values from -0.21875 to 0.21875
- triple_first: float32 [3, 768, 768], P(None, 'dp', 'mp'), may hold values from -144 to 144
- triple_second: float32 [3, 768, 768], P(None, 'dp', 'mp'), may hold values from 2211.84 to 8847.36
- query_value_master: float32 [2, 12, 64], P(None, 'mp', 'dp'), may hold values from -1.5 to 1.5
- query_value_first: float32 [2, 12, 64], P(None, 'mp', 'dp'), may hold values from -192 to 192
- query_value_second: float32 [2, 12, 64], P(None, 'mp', 'dp'), may hold values from 3944.448 to 15851.52
- output_master: float32 [768, 768], P('mp', 'dp'), may hold values from -0.875 to 0.875
- output_first: float32 [768, 768], P('mp', 'dp'), may hold values from -57.6 to 57.6
- output_second: float32 [768, 768], P('mp', 'dp'), may hold values from 353.8944 to 1400.832
- expand_master: float32 [768, 3072], P('dp', 'mp'), may hold values from -0.21875 to 0.21875
- expand_first: float32 [768, 3072], P('dp', 'mp'), may hold values from -96 to 96
- expand_second: float32 [768, 3072], P('dp', 'mp'), may hold values from 995.328 to 3944.448
- expand_bias_master: float32 [48, 64], P('mp', 'dp'), may hold values from -1.5 to 1.5
- expand_bias_first: float32 [48, 64], P('mp', 'dp'), may hold values from -96 to 96
- expand_bias_second: float32 [48, 64], P('mp', 'dp'), may hold values from 995.328 to 3944.448
- shrink_master: float32 [3072, 768], P('mp', 'dp'), may hold values from -0.109375 to 0.109375
- shrink_first: float32 [3072, 768], P('mp', 'dp'), may hold values from -192 to 192
- shrink_second: float32 [3072, 768], P('mp', 'dp'), may hold values from 3944.448 to 15851.52
- vector_master: float32 [6, 768], P(None, ('dp', 'mp'))
- vector_first: float32 [6, 768], P(None, ('dp', 'mp')), may hold values from -384 to 384
- vector_second: float32 [6, 768], P(None, ('dp', 'mp')), may hold values from 15851.52 to 62668.8
Outputs:
- block_output: bfloat16 [128, 288, 768], P(('dp', 'mp'))
- input_grad: float32 [128, 288, 768], P(('dp', 'mp'))
- triple_master_new: float32 [3, 768, 768], P(None, 'dp', 'mp')
- triple_first_new: float32 [3, 768, 768], P(None, 'dp', 'mp')
- triple_second_new: float32 [3, 768, 768], P(None, 'dp', 'mp')
- triple_copy: bfloat16 [3, 768, 768], P(None, 'dp', 'mp')
- query_value_master_new: float32 [2, 12, 64], P(None, 'mp', 'dp')
- query_value_first_new: float32 [2, 12, 64], P(None, 'mp', 'dp')
- query_value_second_new: float32 [2, 12, 64], P(None, 'mp', 'dp')
- query_value_copy: bfloat16 [2, 12, 64], P(None, 'mp', 'dp')
- output_master_new: float32 [768, 768], P('mp', 'dp')
- output_first_new: float32 [768, 768], P('mp', 'dp')
- output_second_new: float32 [768, 768], P('mp', 'dp')
- output_copy: bfloat16 [768, 768], P('mp', 'dp')
- expand_master_new: float32 [768, 3072], P('dp', 'mp')
- expand_first_new: float32 [768, 3072], P('dp', 'mp')
- expand_second_new: float32 [768, 3072], P('dp', 'mp')
- expand_copy: bfloat16 [768, 3072], P('dp', 'mp')
- expand_bias_master_new: float32 [48, 64], P('mp', 'dp')
- expand_bias_first_new: float32 [48, 64], P('mp', 'dp')
- expand_bias_second_new: float32 [48, 64], P('mp', 'dp')
- expand_bias_copy: bfloat16 [48, 64], P('mp', 'dp')
- shrink_master_new: float32 [3072, 768], P('mp', 'dp')
- shrink_first_new: float32 [3072, 768], P('mp', 'dp')
- shrink_second_new: float32 [3072, 768], P('mp', 'dp')
- shrink_copy: bfloat16 [3072, 768], P('mp', 'dp')
- vector_master_new: float32 [6, 768], P(None, ('dp', 'mp'))
- vector_first_new: float32 [6, 768], P(None, ('dp', 'mp'))
- vector_second_new: float32 [6, 768], P(None, ('dp', 'mp'))
- vector_copy: bfloat16 [6, 768], P(None, ('dp', 'mp'))
Inputs may be any that keep to these rules, and one draw needn't show every extreme that they name: `segments`: along a row the pair numbers never fall; each pair has 1 to 160 tokens, and each row has one pair of exactly 160.
All inputs are finite; a program needn't handle non-finite values.
Results may differ from a plain program's by a relative error of at most 0.018.
Values may be sent and summed in bfloat16 or wider, within the bound.
A program may use at most 256 MiB of HBM per device.

v0:
```python
import jax
import jax.numpy as jnp
from jax import lax
from jax.sharding import PartitionSpec as P

D = 768
HEAD = 64
FF = 3072
STEP = 10
NORM_EPS = 1e-05
BETA_ONE = 0.5
BETA_TWO = 0.6
ADAM_EPS = 1e-08
WEIGHT_DECAY = 0.01
MASKED = -1e30
SQRT_HALF = 0.7071067811865476
INV_ROOT_TAU = 0.3989422804014327


def norm_forward(summed, gain, shift):
    centre = summed - jnp.mean(summed, axis=-1, keepdims=True)
    scale = lax.rsqrt(jnp.mean(centre * centre, axis=-1, keepdims=True) + NORM_EPS)
    normed = centre * scale
    return (gain * normed + shift, normed, scale)


def norm_backward(gradient, gain, normed, scale):
    scaled = gradient * gain
    centred = scaled - jnp.mean(scaled, axis=-1, keepdims=True)
    return scale * (centred - normed * jnp.mean(scaled * normed, axis=-1, keepdims=True))


def adam_update(master, first, second, gradient, rate):
    first_new = BETA_ONE * first + (1.0 - BETA_ONE) * gradient
    second_new = BETA_TWO * second + (1.0 - BETA_TWO) * gradient * gradient
    corrected = first_new / (1.0 - BETA_ONE**STEP)
    spread = jnp.sqrt(second_new / (1.0 - BETA_TWO**STEP))
    master_new = master - rate * (corrected / (spread + ADAM_EPS) + WEIGHT_DECAY * master)
    return (master_new, first_new, second_new, master_new.astype(jnp.bfloat16))


def gather_weight(shard, rows_axis):
    count = lax.axis_size("dp")
    piece = shard.shape[rows_axis] // count
    own = lax.dynamic_slice_in_dim(shard, lax.axis_index("dp") * piece, piece, rows_axis)
    return own


def mm(a, b, dims):
    return lax.dot_general(a, b, (dims, ((), ())), preferred_element_type=jnp.float32)


def per_device(
    activations,
    cotangent,
    segments,
    triple_weight,
    query_value_bias,
    output_weight,
    expand_weight,
    expand_bias,
    shrink_weight,
    vector_params,
    *state
):
    rows, length, _ = activations.shape
    tokens = rows * length
    triple = gather_weight(triple_weight, 1)
    triple = lax.all_gather(
        lax.all_gather(triple, "mp", axis=2, tiled=True), "dp", axis=1, tiled=True
    )
    output = gather_weight(output_weight, 1)
    output = lax.all_gather(
        lax.all_gather(output, "mp", axis=0, tiled=True), "dp", axis=1, tiled=True
    )
    expand = gather_weight(expand_weight, 0)
    expand = lax.all_gather(
        lax.all_gather(expand, "mp", axis=1, tiled=True), "dp", axis=0, tiled=True
    )
    shrink = gather_weight(shrink_weight, 1)
    shrink = lax.all_gather(
        lax.all_gather(shrink, "mp", axis=0, tiled=True), "dp", axis=1, tiled=True
    )
    biases = (
        lax.all_gather(query_value_bias, "mp", axis=1, tiled=True).reshape(2, D).astype(jnp.float32)
    )
    expand_shift = (
        lax.all_gather(expand_bias, "mp", axis=0, tiled=True).reshape(-1).astype(jnp.float32)
    )
    gains = vector_params.astype(jnp.float32)
    heads = D // HEAD
    seg = lax.dynamic_slice_in_dim(segments, lax.axis_index("mp") * rows, rows, 0)
    allowed = (seg[:, :, None] == seg[:, None, :])[:, None]
    x = activations.reshape(tokens, D)
    back = cotangent.reshape(tokens, D).astype(jnp.float32)

    def split(t):
        return t.reshape(rows, length, heads, HEAD)

    query = (mm(x, triple[0], ((1,), (0,))) + biases[0]).astype(jnp.bfloat16)
    key = mm(x, triple[1], ((1,), (0,))).astype(jnp.bfloat16)
    value = (mm(x, triple[2], ((1,), (0,))) + biases[1]).astype(jnp.bfloat16)
    q4, k4, v4 = (split(query), split(key), split(value))
    scores = jnp.einsum("rqhc,rkhc->rhqk", q4, k4, preferred_element_type=jnp.float32) * HEAD ** (
        -0.5
    )
    scores = jnp.where(allowed, scores, MASKED)
    row_max = jnp.max(scores, axis=-1, keepdims=True)
    weights = jnp.exp(scores - row_max)
    probs = weights / jnp.sum(weights, axis=-1, keepdims=True)
    probs_low = probs.astype(jnp.bfloat16)
    context = jnp.einsum("rhqk,rkhc->rqhc", probs_low, v4, preferred_element_type=jnp.float32)
    context = context.astype(jnp.bfloat16).reshape(tokens, D)
    attended = mm(context, output, ((1,), (0,)))
    mixed = x.astype(jnp.float32) + attended + gains[2]
    hidden, normed_one, scale_one = norm_forward(mixed, gains[0], gains[1])
    hidden_low = hidden.astype(jnp.bfloat16)
    expanded = mm(hidden_low, expand, ((1,), (0,))) + expand_shift
    cumulative = 0.5 * (1.0 + jax.scipy.special.erf(expanded * SQRT_HALF))
    active = (expanded * cumulative).astype(jnp.bfloat16)
    slope = (cumulative + expanded * jnp.exp(-0.5 * expanded * expanded) * INV_ROOT_TAU).astype(
        jnp.bfloat16
    )
    shrunk = mm(active, shrink, ((1,), (0,)))
    summed = hidden + shrunk + gains[5]
    result, normed_two, scale_two = norm_forward(summed, gains[3], gains[4])
    dsummed = norm_backward(back, gains[3], normed_two, scale_two)
    dsummed_low = dsummed.astype(jnp.bfloat16)

    def reduce_grad(part):
        part = part.astype(jnp.bfloat16)
        part = lax.psum_scatter(part, "dp", scatter_dimension=part.ndim - 2, tiled=True)
        return lax.psum_scatter(part, "mp", scatter_dimension=part.ndim - 1, tiled=True).astype(
            jnp.float32
        )

    shrink_grad = reduce_grad(mm(dsummed_low, active, ((0,), (0,))))
    dactive = mm(dsummed_low, shrink, ((1,), (1,)))
    dexpanded = (dactive * slope).astype(jnp.bfloat16)
    expand_grad = reduce_grad(mm(hidden_low, dexpanded, ((0,), (0,))))
    dhidden = dsummed + mm(dexpanded, expand, ((1,), (1,)))
    dmixed = norm_backward(dhidden, gains[0], normed_one, scale_one)
    dmixed_low = dmixed.astype(jnp.bfloat16)
    output_grad = reduce_grad(mm(dmixed_low, context, ((0,), (0,))))
    dcontext = split(mm(dmixed_low, output, ((1,), (1,))).astype(jnp.bfloat16))
    dvalue = jnp.einsum("rhqk,rqhc->rkhc", probs_low, dcontext, preferred_element_type=jnp.float32)
    dprobs = jnp.einsum("rqhc,rkhc->rhqk", dcontext, v4, preferred_element_type=jnp.float32)
    inner = jnp.sum(probs * dprobs, axis=-1, keepdims=True)
    dscores = (probs * (dprobs - inner)).astype(jnp.bfloat16)
    dquery = jnp.einsum(
        "rhqk,rkhc->rqhc", dscores, k4, preferred_element_type=jnp.float32
    ) * HEAD ** (-0.5)
    dkey = jnp.einsum(
        "rhqk,rqhc->rkhc", dscores, q4, preferred_element_type=jnp.float32
    ) * HEAD ** (-0.5)
    dthree = [t.astype(jnp.bfloat16).reshape(tokens, D) for t in (dquery, dkey, dvalue)]
    triple_grad = reduce_grad(jnp.stack([mm(x, t, ((0,), (0,))) for t in dthree]))
    input_grad = dmixed
    for j in range(3):
        input_grad = input_grad + mm(dthree[j], triple[j], ((1,), (1,)))

    def total(t):
        return jnp.sum(t.astype(jnp.float32), axis=0)

    vector_grad = jnp.stack(
        [
            total(dhidden * normed_one),
            total(dhidden),
            total(dmixed),
            total(back * normed_two),
            total(back),
            total(dsummed),
            total(dthree[0]),
            total(dthree[2]),
        ]
    )
    vector_grad = lax.psum(
        jnp.concatenate([vector_grad, total(dexpanded).reshape(4, D)]), ("dp", "mp")
    )
    dp, mp = (lax.axis_index("dp"), lax.axis_index("mp"))
    groups, parts = (lax.axis_size("mp"), lax.axis_size("dp"))
    width = D // (groups * parts)
    vec = lax.dynamic_slice_in_dim(vector_grad[:6], (dp * groups + mp) * width, width, 1)
    qv = vector_grad[6:8].reshape(2, heads, HEAD)
    qv = lax.dynamic_slice_in_dim(qv, mp * (heads // groups), heads // groups, 1)
    qv = lax.dynamic_slice_in_dim(qv, dp * (HEAD // parts), HEAD // parts, 2)
    eb = vector_grad[8:].reshape(FF // HEAD, HEAD)
    eb = lax.dynamic_slice_in_dim(eb, mp * (FF // HEAD // groups), FF // HEAD // groups, 0)
    eb = lax.dynamic_slice_in_dim(eb, dp * (HEAD // parts), HEAD // parts, 1)
    grads = (triple_grad, qv, output_grad.T, expand_grad, eb, shrink_grad.T, vec)
    rates = (D ** (-0.5), 0.5, (D // 16) ** (-0.5), D ** (-0.5), 0.5, FF ** (-0.5), 0.3)
    outs = (
        result.astype(jnp.bfloat16).reshape(activations.shape),
        input_grad.reshape(activations.shape),
    )
    for i in range(7):
        outs = outs + adam_update(
            state[3 * i], state[3 * i + 1], state[3 * i + 2], grads[i], rates[i]
        )
    return outs


STATE_SPECS = (
    P(None, "dp", "mp"),
    P(None, "mp", "dp"),
    P("mp", "dp"),
    P("dp", "mp"),
    P("mp", "dp"),
    P("mp", "dp"),
    P(None, ("dp", "mp")),
)


def solution(mesh):
    rows = P(("dp", "mp"), None, None)
    placed = (
        rows,
        rows,
        P("dp", None),
        P(None, None, "mp"),
        P(None, "mp", None),
        P("mp", None),
        P(None, "mp"),
        P("mp", None),
        P("mp", None),
        P(),
    )
    for spec in STATE_SPECS:
        placed = placed + (spec,) * 3
    out_specs = (rows, rows)
    for spec in STATE_SPECS:
        out_specs = out_specs + (spec,) * 4
    return jax.shard_map(
        per_device, mesh=mesh, in_specs=placed, out_specs=out_specs, check_vma=False
    )
```

profile of v0, /device:TPU:0, one launch (start us, length us, event | category | flops | bytes accessed | tf_op | source)
XLA Modules:
  0.0 650.2 jit_solution(2121431900021771325)
XLA Ops:
  8.6 21.7 %all_gather.30 = bf16[3,96,768]{1,0,2:T(4,128)(2,1)} all-gather(bf16[3,96,192]{1,0,2:T(4,128)(2,1)S(1)} %copy.234), channel_id=1, replica_groups=mesh['dp'=8,'mp'=4] {'mp'}, dimensions={2}, use_global_device_ids=true | all-gather | bytes 552960 | tf_op jit(solution)/shard_map/all_gather | solution.py:70
  30.3 2.2 copy.179
  33.6 13.6 %all_gather.33 = bf16[768,96]{1,0:T(8,128)(2,1)S(1)} all-gather(bf16[192,96]{1,0:T(8,128)(2,1)S(1)} %constant_dynamic-slice_fusion.2), channel_id=1, replica_groups=mesh['dp'=8,'mp'=4] {'mp'}, dimensions={0}, use_global_device_ids=true | all-gather | bytes 184320 | tf_op jit(solution)/shard_map/all_gather | solution.py:74
  48.1 17.4 %all_gather.35 = bf16[96,3072]{1,0:T(8,128)(2,1)} all-gather(bf16[96,768]{1,0:T(8,128)(2,1)S(1)} %constant_dynamic-slice_fusion.1), channel_id=1, replica_groups=mesh['dp'=8,'mp'=4] {'mp'}, dimensions={1}, use_global_device_ids=true | all-gather | bytes 737280 | tf_op jit(solution)/shard_map/all_gather | solution.py:78
  66.9 15.8 %all_gather.38 = bf16[3072,96]{0,1:T(8,128)(2,1)} all-gather(bf16[768,96]{0,1:T(8,128)(2,1)S(1)} %copy.235), channel_id=1, replica_groups=mesh['dp'=8,'mp'=4] {'mp'}, dimensions={0}, use_global_device_ids=true | all-gather | bytes 737280 | tf_op jit(solution)/shard_map/all_gather | solution.py:82
  82.8 11.9 %all_gather.32 = bf16[2,12,64]{2,0,1:T(2,128)(2,1)S(1)} all-gather(bf16[2,3,64]{2,0,1:T(2,128)(2,1)S(1)} %copy-done.35), channel_id=1, replica_groups=mesh['dp'=8,'mp'=4] {'mp'}, dimensions={1}, use_global_device_ids=true | all-gather | bytes 3840 | tf_op jit(solution)/shard_map/all_gather | solution.py:85
  96.0 13.1 %all-gather = bf16[4,12,64]{2,1,0:T(8,128)(2,1)S(1)} all-gather(bf16[1,12,64]{2,1,0:T(8,128)(2,1)S(1)} %bitcast.132), channel_id=1, replica_groups=mesh['dp'=8,'mp'=4] {'mp'}, dimensions={0}, use_global_device_ids=true | all-gather | bytes 7680 | tf_op jit(solution)/shard_map/all_gather | solution.py:88
  110.8 4.9 fusion.27
  115.7 4.8 reshape.182
  120.5 5.6 fusion.29
  126.1 5.7 reshape.183
  131.8 5.0 fusion.28
  136.8 5.6 reshape.181
  142.4 11.9 %fusion.36 = f32[4,12,288,288]{2,3,1,0:T(8,128)} fusion(bf16[4,288,12,64]{1,0,3,2:T(4,128)(2,1)} %reshape.183, bf16[4,288,12,64]{1,0,3,2:T(4,128)(2,1)S(1)} %reshape.182), kind=kOutput, calls=%fused_computation.80 | convolution fusion | flops 509607936 | bytes 19464192 | tf_op jit(solution)/shard_map/rqhc,rkhc->rhqk/dot_general | solution.py:104
  154.3 25.5 %fusion.85 = (f32[4,12,288]{2,1,0:T(8,128)S(1)}, f32[4,12,288,288]{2,3,1,0:T(8,128)}) fusion(f32[4,12,288,288]{2,3,1,0:T(8,128)} %fusion.36, pred[4,288,288]{1,2,0:T(8,128)(4,1)S(1)} %broadcast_compare_fusion), kind=kOutput, calls=%fused_computation.169 | output fusion | flops 23888160 | bytes 32237568 | tf_op jit(solution)/shard_map/sub | solution.py:109
  179.8 9.3 %convert_bitcast_fusion.1 = bf16[4,288,12,64]{1,3,2,0:T(8,128)(2,1)S(1)} fusion(bf16[4,288,12,64]{1,0,3,2:T(4,128)(2,1)S(1)} %copy-done.15, f32[4,12,288,288]{2,3,1,0:T(8,128)} %get-tuple-element.200, f32[4,12,288]{2,1,0:T(8,128)S(1)} %get-tuple-element.199), kind=kOutput, calls=%fused_computation.75 | convolution fusion | flops 518455296 | bytes 19519488 | tf_op jit(solution)/shard_map/rhqk,rkhc->rqhc/dot_general | solution.py:112
  189.1 1.8 copy.184
  190.9 2.7 reshape.184
  193.6 4.2 fusion.86
  197.9 1.8 copy-done.9
  200.3 13.7 %multiply_convert_fusion.1 = (bf16[1152,3072]{1,0:T(8,128)(2,1)}, f32[1152,3072]{1,0:T(8,128)}) fusion(f32[3072]{0:T(1024)S(1)} %reshape.194, bf16[768,3072]{1,0:T(8,128)(2,1)} %all-gather.10.cloned.1.call-done, f32[1152,768]{1,0:T(8,128)} %copy-done.9, f32[768]{0:T(1024)S(1)} %get-tuple-element.161, f32[1152]{0:T(1024)S(1)} %add_rsqrt_fusion.1, ...), kind=kOutput, calls=%fused_computation.14 | convolution fusion | flops 5461475328 | bytes 29518848 | tf_op jit(solution)/shard_map/dot_general | solution.py:50
  214.0 11.8 %fusion.87 = (f32[1152]{0:T(1024)S(1)}, f32[1152,768]{1,0:T(8,128)S(1)}) fusion(f32[768]{0:T(1024)S(1)} %get-tuple-element.160, bf16[1152,3072]{1,0:T(8,128)(2,1)} %get-tuple-element.203, bf16[3072,768]{0,1:T(8,128)(2,1)} %all-gather.12.cloned.1.call-done, f32[768]{0:T(1024)S(1)} %get-tuple-element.161, f32[1152]{0:T(1024)S(1)} %add_rsqrt_fusion.1, ...), kind=kOutput, calls=%fused_computation.171 | convolution fusion | flops 5442010112 | bytes 18897408 | tf_op jit(solution)/shard_map/dot_general | solution.py:50
  227.3 1.9 fusion.23
  229.2 3.1 fusion.81
  232.3 16.6 %convert_reduce_fusion = (f32[3072]{0:T(1024)}, bf16[1152,3072]{1,0:T(8,128)(2,1)}) fusion(f32[1152,3072]{1,0:T(8,128)} %get-tuple-element.204, bf16[3072,768]{0,1:T(8,128)(2,1)S(1)} %copy-done.36, f32[1152,768]{1,0:T(8,128)S(1)} %get-tuple-element.184), kind=kOutput, calls=%fused_computation.13 | convolution fusion | flops 5486244864 | bytes 29503488 | tf_op jit(solution)/shard_map/dot_general | solution.py:50
  249.0 9.7 %multiply_reduce_fusion.1 = (f32[768]{0:T(1024)}, f32[1152]{0:T(1024)S(1)}, f32[1152]{0:T(1024)S(1)}, f32[768]{0:T(1024)}, f32[1152,768]{1,0:T(8,128)S(1)}) fusion(f32[1152,768]{1,0:T(8,128)S(1)} %copy-done.10, f32[1152]{0:T(1024)S(1)} %add_rsqrt_fusion.1, f32[1152]{0:T(1024)S(1)} %broadcast_multiply_fusion.4, f32[768]{0:T(1024)S(1)} %get-tuple-element.163, ...), kind=kOutput, calls=%fused_computation.54 | convolution fusion | flops 5444661248 | bytes 22440960 | tf_op jit(solution)/shard_map/dot_general | solution.py:50
  258.7 1.8 fusion.83
  260.5 1.8 copy-done.12
  263.8 4.7 reshape.204
  268.5 6.1 copy.188
  274.6 12.8 %convert_reduce_fusion.1 = (f32[12,64]{1,0:T(8,128)}, bf16[4,288,12,64]{1,3,2,0:T(8,128)(2,1)}) fusion(bf16[4,288,12,64]{1,3,2,0:T(8,128)(2,1)S(1)} %copy.188, f32[4,12,288,288]{2,3,1,0:T(8,128)} %get-tuple-element.200, f32[4,12,288]{2,1,0:T(8,128)S(1)} %get-tuple-element.199), kind=kOutput, calls=%fused_computation.28 | convolution fusion | flops 520224000 | bytes 19522560 | tf_op jit(solution)/shard_map/rhqk,rqhc->rkhc/dot_general | solution.py:146
  287.4 18.2 %multiply_reduce_fusion = (f32[4,12,288]{2,1,0:T(8,128)S(1)}, f32[4,12,288,288]{2,3,1,0:T(8,128)}) fusion(f32[4,12,288,288]{2,3,1,0:T(8,128)} %get-tuple-element.200, f32[4,12,288]{2,1,0:T(8,128)S(1)} %get-tuple-element.199, bf16[4,288,12,64]{1,3,2,0:T(8,128)(2,1)S(1)} %copy.188, bf16[4,288,12,64]{1,0,3,2:T(4,128)(2,1)} %reshape.181), kind=kOutput, calls=%fused_computation.2 | convolution fusion | flops 521538048 | bytes 35500032 | tf_op jit(solution)/shard_map/rqhc,rkhc->rhqk/dot_general | solution.py:147
  305.6 5.3 convolution_convert_fusion.4
  310.9 14.6 %multiply_convert_fusion = bf16[4,12,288,288]{2,3,1,0:T(8,128)(2,1)S(1)} fusion(f32[4,12,288,288]{2,3,1,0:T(8,128)} %get-tuple-element.209, f32[4,12,288]{2,1,0:T(8,128)S(1)} %get-tuple-element.208, f32[4,12,288,288]{2,3,1,0:T(8,128)} %get-tuple-element.200, f32[4,12,288]{2,1,0:T(8,128)S(1)} %get-tuple-element.199), kind=kLoop, calls=%fused_computation.1 | loop fusion | flops 15925248 | bytes 39923712 | tf_op jit(solution)/shard_map/convert_element_type | solution.py:149
  325.6 4.0 copy-done.2
  329.6 3.6 convert_reduce_fusion.2
  333.3 9.4 %fusion.31 = bf16[4,288,12,64]{1,3,2,0:T(8,128)(2,1)} fusion(bf16[4,12,288,288]{2,3,1,0:T(8,128)(2,1)} %copy-done.2, bf16[4,288,12,64]{1,0,3,2:T(4,128)(2,1)S(1)} %copy-done.4), kind=kOutput, calls=%fused_computation.73 | convolution fusion | flops 511377408 | bytes 11501568 | tf_op jit(solution)/shard_map/rhqk,rqhc->rkhc/dot_general | solution.py:153
  342.7 3.2 copy.198
  345.9 5.0 reshape.189
  350.9 3.2 copy.195
  354.2 4.8 reshape.188
  359.0 3.2 copy.192
  362.3 4.8 reshape.187
  367.1 3.3 fusion.48
  372.1 1.7 fusion.46
  373.8 2.0 pad_maximum_fusion
  375.8 8.1 %copy.228 = bf16[3,768,768]{2,0,1:T(4,128)(2,1)} copy(bf16[3,768,768]{1,2,0:T(8,128)(2,1)} %pad_maximum_fusion) | data formatting | bytes 7077888
  384.0 4.9 copy.237
  389.6 12.2 %convolution_convert_fusion.1 = bf16[768,3072]{1,0:T(8,128)(2,1)} fusion(bf16[1152,3072]{1,0:T(8,128)(2,1)} %get-tuple-element.215, f32[1152,768]{1,0:T(8,128)} %copy-done.9, f32[768]{0:T(1024)S(1)} %copy-done.34, f32[1152]{0:T(1024)S(1)} %copy-done.25, f32[1152]{0:T(1024)S(1)} %broadcast_multiply_fusion.4, f32[768]{0:T(1024)S(1)} %copy-done.30), kind=kOutput, calls=%fused_computation.27 | convolution fusion | flops 5442600960 | bytes 15350784 | tf_op jit(solution)/shard_map/dot_general | solution.py:50
  401.9 11.1 %convolution_convert_fusion = bf16[768,3072]{1,0:T(8,128)(2,1)} fusion(bf16[1152,3072]{1,0:T(8,128)(2,1)} %get-tuple-element.203, f32[1152,768]{1,0:T(8,128)} %copy-done.13), kind=kOutput, calls=%fused_computation.26 | convolution fusion | flops 5439062016 | bytes 15335424 | tf_op jit(solution)/shard_map/dot_general | solution.py:50
  413.1 1.8 copy.230
  415.0 20.5 %reduce-scatter.25.cloned.1.call-done = bf16[96,2304]{1,0:T(8,128)(2,1)} async-done(((bf16[768,2304]{1,0:T(8,128)(2,1)}), bf16[96,2304]{1,0:T(8,128)(2,1)}) %reduce-scatter.25.cloned.1.call-update) | async-done | bytes 442384
  438.7 1.8 copy.202
  447.3 39.7 %psum.7 = f32[12,768]{1,0:T(8,128)S(1)} all-reduce(f32[12,768]{1,0:T(8,128)S(1)} %concatenate.3), channel_id=1, replica_groups=mesh['dp'=8,'mp'=4] {'dp','mp'}, use_global_device_ids=true, to_apply=%region_22.23 | all-reduce | flops 9216 | bytes 73728 | tf_op jit(solution)/shard_map/psum | solution.py:177
  495.2 4.6 convolution_add_fusion.5
  499.9 4.7 convolution_add_fusion.4
  504.6 46.3 %reduce-scatter.21.cloned.1.call-done = bf16[96,3072]{1,0:T(8,128)(2,1)} async-done(((bf16[768,3072]{1,0:T(8,128)(2,1)}), bf16[96,3072]{1,0:T(8,128)(2,1)}) %reduce-scatter.21.cloned.1.call-update) | async-done | bytes 589840 | tf_op jit(solution)/shard_map/reduce_scatter | solution.py:132
  550.9 5.8 convolution_add_fusion.3
  556.6 16.5 %reduce-scatter.27.cloned.1.call-done = bf16[192,96]{1,0:T(8,128)(2,1)} async-done(((bf16[768,96]{1,0:T(8,128)(2,1)}), bf16[192,96]{1,0:T(8,128)(2,1)}) %reduce-scatter.27.cloned.1.call-update) | async-done | bytes 36880
  577.1 18.5 %reduce-scatter.13.cloned.1.call-done = bf16[3,96,192]{1,2,0:T(8,128)(2,1)} async-done(((bf16[3,96,768]{1,2,0:T(8,128)(2,1)}), bf16[3,96,192]{1,2,0:T(8,128)(2,1)}) %reduce-scatter.13.cloned.1.call-update) | async-done | bytes 110608 | tf_op jit(solution)/shard_map/reduce_scatter | solution.py:133
  600.3 17.9 %reduce-scatter.19.cloned.1.call-done = bf16[96,768]{1,0:T(8,128)(2,1)} async-done(((bf16[96,3072]{1,0:T(8,128)(2,1)}), bf16[96,768]{1,0:T(8,128)(2,1)}) %reduce-scatter.19.cloned.1.call-update) | async-done | bytes 147472 | tf_op jit(solution)/shard_map/reduce_scatter | solution.py:133
  618.2 2.2 fusion.76
  620.4 20.3 %reduce-scatter.23.cloned.1.call-done = bf16[96,768]{1,0:T(8,128)(2,1)} async-done(((bf16[96,3072]{1,0:T(8,128)(2,1)}), bf16[96,768]{1,0:T(8,128)(2,1)}) %reduce-scatter.23.cloned.1.call-update) | async-done | bytes 147472 | tf_op jit(solution)/shard_map/reduce_scatter | solution.py:133
  640.7 2.4 fusion.72
  (181 shorter events, 40.7 us)
Async XLA Ops:
  7.2 40.9 %copy-start = (bf16[768,768]{1,0:T(8,128)(2,1)S(1)}, bf16[768,768]{1,0:T(8,128)(2,1)}, u32[]{:S(2)}) copy-start(bf16[768,768]{1,0:T(8,128)(2,1)} %param.37) | copy-start | bytes 3538948
  7.2 103.6 %all-gather.6.cloned.1.call-start = ((), (), s32[]{:S(2)}) async-start(), calls=%async_computation.8 | async-start | bytes 3981312 | tf_op jit(solution)/shard_map/all_gather | solution.py:69
  8.6 74.2 %copy-start.35 = (bf16[2,3,64]{2,0,1:T(2,128)(2,1)S(1)}, bf16[2,3,64]{2,0,1:T(2,128)(2,1)}, u32[]{:S(2)}) copy-start(bf16[2,3,64]{2,0,1:T(2,128)(2,1)} %param.35) | copy-start | bytes 2308
  30.3 65.6 %copy-start.31 = (bf16[6,768]{1,0:T(8,128)(2,1)S(1)}, bf16[6,768]{1,0:T(8,128)(2,1)}, u32[]{:S(2)}) copy-start(bf16[6,768]{1,0:T(8,128)(2,1)} %param.40) | copy-start | bytes 27652
  30.3 65.7 %copy-start.32 = (bf16[12,64]{1,0:T(8,128)(2,1)S(1)}, bf16[12,64]{1,0:T(8,128)(2,1)}, u32[]{:S(2)}) copy-start(bf16[12,64]{1,0:T(8,128)(2,1)} %param.38) | copy-start | bytes 4612
  30.3 78.9 %copy-start.6 = (bf16[4,288,768]{2,1,0:T(8,128)(2,1)S(1)}, bf16[4,288,768]{2,1,0:T(8,128)(2,1)}, u32[]{:S(2)}) copy-start(bf16[4,288,768]{2,1,0:T(8,128)(2,1)} %param.32) | copy-start | bytes 5308420
  32.6 161.1 %all-gather.8.cloned.1.call-start = ((), (), s32[]{:S(2)}) async-start(), calls=%async_computation.9 | async-start | bytes 1327104 | tf_op jit(solution)/shard_map/all_gather | solution.py:73
  48.0 152.2 %all-gather.10.cloned.1.call-start = ((), (), s32[]{:S(2)}) async-start(), calls=%async_computation.10 | async-start | bytes 5308416 | tf_op jit(solution)/shard_map/all_gather | solution.py:77
  65.6 148.4 %all-gather.12.cloned.1.call-start = ((), (), s32[]{:S(2)}) async-start(), calls=%async_computation.11 | async-start | bytes 5308416 | tf_op jit(solution)/shard_map/all_gather | solution.py:81
  82.7 330.3 %reduce-scatter.15.cloned.1.call-start = ((), (), s32[]{:S(2)}) async-start(), calls=%async_computation.13 | async-start | bytes 1327104 | tf_op jit(solution)/shard_map/reduce_scatter | solution.py:132
  95.9 118.1 %copy-start.33 = (f32[768]{0:T(1024)}, f32[768]{0:T(1024)S(1)}, u32[]{:S(2)}) copy-start(f32[768]{0:T(1024)S(1)} %get-tuple-element.161) | copy-start | bytes 9220
  96.0 162.7 %copy-start.29 = (f32[768]{0:T(1024)}, f32[768]{0:T(1024)S(1)}, u32[]{:S(2)}) copy-start(f32[768]{0:T(1024)S(1)} %get-tuple-element.163) | copy-start | bytes 9220
  120.5 21.9 %copy-start.3 = (bf16[4,288,12,64]{1,0,3,2:T(4,128)(2,1)}, bf16[4,288,12,64]{1,0,3,2:T(4,128)(2,1)S(1)}, u32[]{:S(2)}) copy-start(bf16[4,288,12,64]{1,0,3,2:T(4,128)(2,1)S(1)} %reshape.182) | copy-start | bytes 5308420
  154.3 25.5 %copy-start.15 = (bf16[4,288,12,64]{1,0,3,2:T(4,128)(2,1)S(1)}, bf16[4,288,12,64]{1,0,3,2:T(4,128)(2,1)}, u32[]{:S(2)}) copy-start(bf16[4,288,12,64]{1,0,3,2:T(4,128)(2,1)} %reshape.181) | copy-start | bytes 5308420
  197.8 1.8 copy-start.9
  200.2 58.4 %copy-start.24 = (f32[1152]{0:T(1024)}, f32[1152]{0:T(1024)S(1)}, u32[]{:S(2)}) copy-start(f32[1152]{0:T(1024)S(1)} %add_rsqrt_fusion.1) | copy-start | bytes 13828
  225.8 1.5 copy-start.7
  229.2 3.1 copy-start.36
  229.2 19.7 %slice-start = ((s8[4718592]{0:T(1024)(128)(4,1)}), s8[4194304]{0:T(1024)(128)(4,1)S(1)}, s32[]{:S(2)}) async-start(s8[4718592]{0:T(1024)(128)(4,1)} %bitcast.133), calls=%async_computation.20 | async-start | bytes 8388608
  232.3 16.7 %copy-start.13 = (f32[1152,768]{1,0:T(8,128)}, f32[1152,768]{1,0:T(8,128)S(1)}, u32[]{:S(2)}) copy-start(f32[1152,768]{1,0:T(8,128)S(1)} %get-tuple-element.184) | copy-start | bytes 10616836
  232.3 16.7 %copy-start.10 = (f32[1152,768]{1,0:T(8,128)S(1)}, f32[1152,768]{1,0:T(8,128)}, u32[]{:S(2)}) copy-start(f32[1152,768]{1,0:T(8,128)} %copy-done.9) | copy-start | bytes 10616836
  232.3 16.7 %slice-start.1 = ((s8[4718592]{0:T(1024)(128)(4,1)}), s8[524288]{0:T(1024)(128)(4,1)S(1)}, s32[]{:S(2)}) async-start(s8[4718592]{0:T(1024)(128)(4,1)} %bitcast.133), calls=%async_computation.21 | async-start | bytes 1048576
  258.7 3.6 copy-start.38
  260.5 1.8 copy-start.12
  310.9 18.6 %copy-start.5 = (bf16[4,288,12,64]{1,0,3,2:T(4,128)(2,1)S(1)}, bf16[4,288,12,64]{1,0,3,2:T(4,128)(2,1)}, u32[]{:S(2)}) copy-start(bf16[4,288,12,64]{1,0,3,2:T(4,128)(2,1)} %reshape.183) | copy-start | bytes 5308420
  325.6 4.0 copy-start.2
  329.6 3.7 copy-start.4
  333.2 102.3 %reduce-scatter.25.cloned.1.call-start = ((), (), s32[]{:S(2)}) async-start(), calls=%async_computation.18 | async-start | bytes 3981312
  333.3 9.4 %copy-start.14 = (bf16[4,288,12,64]{1,3,2,0:T(8,128)(2,1)S(1)}, bf16[4,288,12,64]{1,3,2,0:T(8,128)(2,1)}, u32[]{:S(2)}) copy-start(bf16[4,288,12,64]{1,3,2,0:T(8,128)(2,1)} %get-tuple-element.213) | copy-start | bytes 5308420
  342.7 8.3 %copy-start.8 = (bf16[4,288,12,64]{1,3,2,0:T(8,128)(2,1)S(1)}, bf16[4,288,12,64]{1,3,2,0:T(8,128)(2,1)}, u32[]{:S(2)}) copy-start(bf16[4,288,12,64]{1,3,2,0:T(8,128)(2,1)} %fusion.31) | copy-start | bytes 5308420
  354.2 4.8 copy-start.11
  362.3 4.8 copy-start.16
  367.1 3.3 copy-start.17
  367.1 3.4 copy-start.37
  370.4 1.7 copy-start.19
  388.9 0.7 copy-start.25
  388.9 0.7 copy-start.30
  388.9 0.7 copy-start.34
  388.9 104.6 %reduce-scatter.17.cloned.1.call-start = ((), (), s32[]{:S(2)}) async-start(), calls=%async_computation.14 | async-start | bytes 5308416 | tf_op jit(solution)/shard_map/reduce_scatter | solution.py:132
  401.8 149.0 %reduce-scatter.21.cloned.1.call-start = ((), (), s32[]{:S(2)}) async-start(), calls=%async_computation.16 | async-start | bytes 5308416 | tf_op jit(solution)/shard_map/reduce_scatter | solution.py:132
  413.0 25.4 %copy-start.26 = (f32[768]{0:T(1024)S(1)}, f32[768]{0:T(1024)}, u32[]{:S(2)}) copy-start(f32[768]{0:T(1024)} %get-tuple-element.156) | copy-start | bytes 9220
  413.0 25.5 %copy-start.20 = (f32[3,96,192]{2,1,0:T(8,128)S(1)}, f32[3,96,192]{2,1,0:T(8,128)}, u32[]{:S(2)}) copy-start(f32[3,96,192]{2,1,0:T(8,128)} %param.42) | copy-start | bytes 663556
  413.0 25.6 %copy-start.21 = (f32[3,96,192]{2,1,0:T(8,128)S(1)}, f32[3,96,192]{2,1,0:T(8,128)}, u32[]{:S(2)}) copy-start(f32[3,96,192]{2,1,0:T(8,128)} %param.43) | copy-start | bytes 663556
  413.0 31.4 %copy-start.28 = (f32[768]{0:T(1024)S(1)}, f32[768]{0:T(1024)}, u32[]{:S(2)}) copy-start(f32[768]{0:T(1024)} %get-tuple-element.185) | copy-start | bytes 9220
  413.0 33.5 %copy-start.27 = (f32[768]{0:T(1024)S(1)}, f32[768]{0:T(1024)}, u32[]{:S(2)}) copy-start(f32[768]{0:T(1024)} %get-tuple-element.183) | copy-start | bytes 9220
  413.0 160.1 %reduce-scatter.27.cloned.1.call-start = ((), (), s32[]{:S(2)}) async-start(), calls=%async_computation.19 | async-start | bytes 245760
  414.9 180.6 %reduce-scatter.13.cloned.1.call-start = ((), (), s32[]{:S(2)}) async-start(), calls=%async_computation.12 | async-start | bytes 737280 | tf_op jit(solution)/shard_map/reduce_scatter | solution.py:133
  438.3 179.8 %reduce-scatter.19.cloned.1.call-start = ((), (), s32[]{:S(2)}) async-start(), calls=%async_computation.15 | async-start | bytes 737280 | tf_op jit(solution)/shard_map/reduce_scatter | solution.py:133
  493.5 147.2 %reduce-scatter.23.cloned.1.call-start = ((), (), s32[]{:S(2)}) async-start(), calls=%async_computation.17 | async-start | bytes 737280 | tf_op jit(solution)/shard_map/reduce_scatter | solution.py:133
  495.2 4.7 copy-start.18
  556.6 61.6 %copy-start.22 = (f32[96,768]{1,0:T(8,128)S(1)}, f32[96,768]{1,0:T(8,128)}, u32[]{:S(2)}) copy-start(f32[96,768]{1,0:T(8,128)} %param.50) | copy-start | bytes 884740
  556.6 61.6 %copy-start.23 = (f32[96,768]{1,0:T(8,128)S(1)}, f32[96,768]{1,0:T(8,128)}, u32[]{:S(2)}) copy-start(f32[96,768]{1,0:T(8,128)} %param.51) | copy-start | bytes 884740
  595.5 47.6 %copy-start.1 = (bf16[768,768]{1,0:T(8,128)(2,1)S(1)}, bf16[768,768]{1,0:T(8,128)(2,1)}, u32[]{:S(2)}) copy-start(bf16[768,768]{1,0:T(8,128)(2,1)} %param.37) | copy-start | bytes 3538948
Sparse Core Ops, SparseCore 0:
  32.7 33.7 all-gather.5
  68.9 24.0 all-gather.7
  94.9 38.9 all-gather.9
  135.6 38.9 all-gather.11
  333.3 35.0 reduce-scatter.14
  389.0 46.4 reduce-scatter.24
  439.3 54.1 reduce-scatter.16
  496.9 53.8 reduce-scatter.20
  553.8 19.3 reduce-scatter.26
  575.3 20.2 reduce-scatter.12
  597.8 20.2 reduce-scatter.18
  620.3 20.3 reduce-scatter.22
where the time goes:
time: 657 us; the launch traced here: 650 us
  matrix products  189 us (29%)
  waiting for transfers between devices  142 us (22%)
  blocking collectives  133 us (20%)
  local copies, waits for them, and re-layouts  109 us (17%)
  other arithmetic  61.6 us (9%)
  between operations  15.1 us (2%)
    dot_general x18, matrix products, mm(): lax.dot_general(a, b, (dims, ((), ())), preferred_element_type=jnp.float32)  124 us
    reduce_scatter x3, waiting for transfers between devices, reduce_grad(): lax.psum_scatter(part, 'mp', scatter_dimension=part.ndim - 1, tiled=True)  56.6 us
    reduce_scatter x3, waiting for transfers between devices, reduce_grad(): lax.psum_scatter(part, 'dp', scatter_dimension=part.ndim - 2, tiled=True)  47.9 us
    unnamed x109, local copies, waits for them, and re-layouts  41.8 us
    psum x1, blocking collectives, per_device(): lax.psum(jnp.concatenate([vector_grad, total(dexpanded).reshape(4, D)]),...  39.7 us
    unnamed x14, waiting for transfers between devices  37.2 us
    reshape x5, local copies, waits for them, and re-layouts, split(): return t.reshape(rows, length, heads, HEAD)  26.8 us
    sub x1, other arithmetic, per_device(): weights = jnp.exp(scores - row_max)  25.5 us
  transfers between devices with their start and end apart: 12, of which 7 were waited for; matrix products, arithmetic and copies ran while one was open for 36% of the time, Pallas kernels for 0%

commit v1 on v0

--- a/solution.py
+++ b/solution.py
@@ -174,8 +174,11 @@
             total(dthree[2]),
         ]
     )
-    vector_grad = lax.psum(
-        jnp.concatenate([vector_grad, total(dexpanded).reshape(4, D)]), ("dp", "mp")
+    vector_grad = jnp.sum(
+        lax.all_gather(
+            jnp.concatenate([vector_grad, total(dexpanded).reshape(4, D)]), ("dp", "mp")
+        ),
+        axis=0,
     )
     dp, mp = (lax.axis_index("dp"), lax.axis_index("mp"))
     groups, parts = (lax.axis_size("mp"), lax.axis_size("dp"))

time: 657 us -> 714 us (1.087)
  waiting for transfers between devices: 142 us -> 241 us
  blocking collectives: 133 us -> 93.6 us
    all_gather x0 -> x1, waiting for transfers between devices: none -> 53.2 us  [per_device(): lax.all_gather(jnp.concatenate([vector_grad, total(dexpanded).reshape(4,...]
    reduce_scatter x3, waiting for transfers between devices: 47.9 us -> 97.6 us  [reduce_grad(): lax.psum_scatter(part, 'dp', scatter_dimension=part.ndim - 2, tiled=True)]
    psum x1 -> x0, blocking collectives: 39.7 us -> none  [per_device(): lax.psum(jnp.concatenate([vector_grad, total(dexpanded).reshape(4, D)]),...]
    unnamed x14 -> x15, waiting for transfers between devices: 37.2 us -> 31.7 us
    unnamed x109 -> x135, local copies, waits for them, and re-layouts: 41.8 us -> 41.9 us
  transfers between devices with their start and end apart: 12 -> 13, of which waited for: 7 -> 8; matrix products, arithmetic and copies ran while one was open for 36% -> 32% of each run, Pallas kernels for 0% -> 0%
where the time goes in v1:
time: 714 us; the launch traced here: 708 us
  waiting for transfers between devices  241 us (34%)
  matrix products  189 us (26%)
  local copies, waits for them, and re-layouts  107 us (15%)
  blocking collectives  93.6 us (13%)
  other arithmetic  61.3 us (9%)
  between operations  14.9 us (2%)
    dot_general x18, matrix products, mm(): lax.dot_general(a, b, (dims, ((), ())), preferred_element_type=jnp.float32)  124 us
    reduce_scatter x3, waiting for transfers between devices, reduce_grad(): lax.psum_scatter(part, 'dp', scatter_dimension=part.ndim - 2, tiled=True)  97.6 us
    reduce_scatter x3, waiting for transfers between devices, reduce_grad(): lax.psum_scatter(part, 'mp', scatter_dimension=part.ndim - 1, tiled=True)  58.7 us
    all_gather x1, waiting for transfers between devices, per_device(): lax.all_gather(jnp.concatenate([vector_grad, total(dexpanded).reshape(4,...  53.2 us
    unnamed x135, local copies, waits for them, and re-layouts  41.9 us
    unnamed x15, waiting for transfers between devices  31.7 us
    reshape x5, local copies, waits for them, and re-layouts, split(): return t.reshape(rows, length, heads, HEAD)  26.8 us
    sub x1, other arithmetic, per_device(): weights = jnp.exp(scores - row_max)  25.9 us
  transfers between devices with their start and end apart: 13, of which 8 were waited for; matrix products, arithmetic and copies ran while one was open for 32% of the time, Pallas kernels for 0%

profile of v1, /device:TPU:0, one launch (start us, length us, event | category | flops | bytes accessed | tf_op | source)
XLA Modules:
  0.0 707.9 jit_solution(9662684756458702172)
XLA Ops:
  8.6 21.7 %all_gather.36 = bf16[3,96,768]{1,0,2:T(4,128)(2,1)} all-gather(bf16[3,96,192]{1,0,2:T(4,128)(2,1)S(1)} %copy.234), channel_id=1, replica_groups=mesh['dp'=8,'mp'=4] {'mp'}, dimensions={2}, use_global_device_ids=true | all-gather | bytes 552960 | tf_op jit(solution)/shard_map/all_gather | solution.py:70
  30.3 2.2 copy.179
  33.6 13.6 %all_gather.39 = bf16[768,96]{1,0:T(8,128)(2,1)S(1)} all-gather(bf16[192,96]{1,0:T(8,128)(2,1)S(1)} %constant_dynamic-slice_fusion.2), channel_id=1, replica_groups=mesh['dp'=8,'mp'=4] {'mp'}, dimensions={0}, use_global_device_ids=true | all-gather | bytes 184320 | tf_op jit(solution)/shard_map/all_gather | solution.py:74
  48.1 17.4 %all_gather.41 = bf16[96,3072]{1,0:T(8,128)(2,1)} all-gather(bf16[96,768]{1,0:T(8,128)(2,1)S(1)} %constant_dynamic-slice_fusion.1), channel_id=1, replica_groups=mesh['dp'=8,'mp'=4] {'mp'}, dimensions={1}, use_global_device_ids=true | all-gather | bytes 737280 | tf_op jit(solution)/shard_map/all_gather | solution.py:78
  66.9 15.8 %all_gather.44 = bf16[3072,96]{0,1:T(8,128)(2,1)} all-gather(bf16[768,96]{0,1:T(8,128)(2,1)S(1)} %copy.235), channel_id=1, replica_groups=mesh['dp'=8,'mp'=4] {'mp'}, dimensions={0}, use_global_device_ids=true | all-gather | bytes 737280 | tf_op jit(solution)/shard_map/all_gather | solution.py:82
  82.8 11.9 %all_gather.38 = bf16[2,12,64]{2,0,1:T(2,128)(2,1)S(1)} all-gather(bf16[2,3,64]{2,0,1:T(2,128)(2,1)S(1)} %copy-done.48), channel_id=1, replica_groups=mesh['dp'=8,'mp'=4] {'mp'}, dimensions={1}, use_global_device_ids=true | all-gather | bytes 3840 | tf_op jit(solution)/shard_map/all_gather | solution.py:85
  96.0 13.1 %all-gather.1 = bf16[4,12,64]{2,1,0:T(8,128)(2,1)S(1)} all-gather(bf16[1,12,64]{2,1,0:T(8,128)(2,1)S(1)} %bitcast.134), channel_id=1, replica_groups=mesh['dp'=8,'mp'=4] {'mp'}, dimensions={0}, use_global_device_ids=true | all-gather | bytes 7680 | tf_op jit(solution)/shard_map/all_gather | solution.py:88
  110.8 4.9 fusion.27
  115.7 4.8 reshape.182
  120.5 5.6 fusion.29
  126.1 5.6 reshape.183
  131.8 5.0 fusion.28
  136.7 5.7 reshape.181
  142.4 11.9 %fusion.36 = f32[4,12,288,288]{2,3,1,0:T(8,128)} fusion(bf16[4,288,12,64]{1,0,3,2:T(4,128)(2,1)} %reshape.183, bf16[4,288,12,64]{1,0,3,2:T(4,128)(2,1)S(1)} %reshape.182), kind=kOutput, calls=%fused_computation.80 | convolution fusion | flops 509607936 | bytes 19464192 | tf_op jit(solution)/shard_map/rqhc,rkhc->rhqk/dot_general | solution.py:104
  154.3 25.9 %fusion.85 = (f32[4,12,288]{2,1,0:T(8,128)S(1)}, f32[4,12,288,288]{2,3,1,0:T(8,128)}) fusion(f32[4,12,288,288]{2,3,1,0:T(8,128)} %fusion.36, pred[4,288,288]{1,2,0:T(8,128)(4,1)S(1)} %broadcast_compare_fusion), kind=kOutput, calls=%fused_computation.169 | output fusion | flops 23888160 | bytes 32237568 | tf_op jit(solution)/shard_map/sub | solution.py:109
  180.2 9.3 %convert_bitcast_fusion.1 = bf16[4,288,12,64]{1,3,2,0:T(8,128)(2,1)S(1)} fusion(bf16[4,288,12,64]{1,0,3,2:T(4,128)(2,1)S(1)} %copy-done.15, f32[4,12,288,288]{2,3,1,0:T(8,128)} %get-tuple-element.200, f32[4,12,288]{2,1,0:T(8,128)S(1)} %get-tuple-element.199), kind=kOutput, calls=%fused_computation.75 | convolution fusion | flops 518455296 | bytes 19519488 | tf_op jit(solution)/shard_map/rhqk,rkhc->rqhc/dot_general | solution.py:112
  189.5 1.8 copy.184
  191.3 2.7 reshape.184
  194.0 4.2 fusion.86
  198.3 1.8 copy-done.9
  200.6 13.8 %multiply_convert_fusion.1 = (bf16[1152,3072]{1,0:T(8,128)(2,1)}, f32[1152,3072]{1,0:T(8,128)}) fusion(f32[3072]{0:T(1024)S(1)} %reshape.194, bf16[768,3072]{1,0:T(8,128)(2,1)} %all-gather.13.cloned.1.call-done, f32[1152,768]{1,0:T(8,128)} %copy-done.9, f32[768]{0:T(1024)S(1)} %get-tuple-element.161, f32[1152]{0:T(1024)S(1)} %add_rsqrt_fusion.1, ...), kind=kOutput, calls=%fused_computation.14 | convolution fusion | flops 5461475328 | bytes 29518848 | tf_op jit(solution)/shard_map/dot_general | solution.py:50
  214.4 11.8 %fusion.87 = (f32[1152]{0:T(1024)S(1)}, f32[1152,768]{1,0:T(8,128)S(1)}) fusion(f32[768]{0:T(1024)S(1)} %get-tuple-element.160, bf16[1152,3072]{1,0:T(8,128)(2,1)} %get-tuple-element.203, bf16[3072,768]{0,1:T(8,128)(2,1)} %all-gather.15.cloned.1.call-done, f32[768]{0:T(1024)S(1)} %get-tuple-element.161, f32[1152]{0:T(1024)S(1)} %add_rsqrt_fusion.1, ...), kind=kOutput, calls=%fused_computation.171 | convolution fusion | flops 5442010112 | bytes 18897408 | tf_op jit(solution)/shard_map/dot_general | solution.py:50
  227.7 1.9 fusion.23
  229.6 3.1 fusion.81
  232.7 16.6 %convert_reduce_fusion = (f32[3072]{0:T(1024)}, bf16[1152,3072]{1,0:T(8,128)(2,1)}) fusion(f32[1152,3072]{1,0:T(8,128)} %get-tuple-element.204, bf16[3072,768]{0,1:T(8,128)(2,1)S(1)} %copy-done.49, f32[1152,768]{1,0:T(8,128)S(1)} %get-tuple-element.184), kind=kOutput, calls=%fused_computation.13 | convolution fusion | flops 5486244864 | bytes 29503488 | tf_op jit(solution)/shard_map/dot_general | solution.py:50
  249.4 9.7 %multiply_reduce_fusion.1 = (f32[768]{0:T(1024)}, f32[1152]{0:T(1024)S(1)}, f32[1152]{0:T(1024)S(1)}, f32[768]{0:T(1024)}, f32[1152,768]{1,0:T(8,128)S(1)}) fusion(f32[1152,768]{1,0:T(8,128)S(1)} %copy-done.10, f32[1152]{0:T(1024)S(1)} %add_rsqrt_fusion.1, f32[1152]{0:T(1024)S(1)} %broadcast_multiply_fusion.4, f32[768]{0:T(1024)S(1)} %get-tuple-element.163, ...), kind=kOutput, calls=%fused_computation.54 | convolution fusion | flops 5444661248 | bytes 22440960 | tf_op jit(solution)/shard_map/dot_general | solution.py:50
  259.1 1.8 fusion.83
  260.9 1.8 copy-done.12
  264.3 4.6 reshape.208
  268.9 6.1 copy.188
  275.0 12.8 %convert_reduce_fusion.1 = (f32[12,64]{1,0:T(8,128)}, bf16[4,288,12,64]{1,3,2,0:T(8,128)(2,1)}) fusion(bf16[4,288,12,64]{1,3,2,0:T(8,128)(2,1)S(1)} %copy.188, f32[4,12,288,288]{2,3,1,0:T(8,128)} %get-tuple-element.200, f32[4,12,288]{2,1,0:T(8,128)S(1)} %get-tuple-element.199), kind=kOutput, calls=%fused_computation.28 | convolution fusion | flops 520224000 | bytes 19522560 | tf_op jit(solution)/shard_map/rhqk,rqhc->rkhc/dot_general | solution.py:146
  287.8 18.1 %multiply_reduce_fusion = (f32[4,12,288]{2,1,0:T(8,128)S(1)}, f32[4,12,288,288]{2,3,1,0:T(8,128)}) fusion(f32[4,12,288,288]{2,3,1,0:T(8,128)} %get-tuple-element.200, f32[4,12,288]{2,1,0:T(8,128)S(1)} %get-tuple-element.199, bf16[4,288,12,64]{1,3,2,0:T(8,128)(2,1)S(1)} %copy.188, bf16[4,288,12,64]{1,0,3,2:T(4,128)(2,1)} %reshape.181), kind=kOutput, calls=%fused_computation.2 | convolution fusion | flops 521538048 | bytes 35500032 | tf_op jit(solution)/shard_map/rqhc,rkhc->rhqk/dot_general | solution.py:147
  305.9 5.3 convolution_convert_fusion.4
  311.2 14.5 %multiply_convert_fusion = bf16[4,12,288,288]{2,3,1,0:T(8,128)(2,1)S(1)} fusion(f32[4,12,288,288]{2,3,1,0:T(8,128)} %get-tuple-element.209, f32[4,12,288]{2,1,0:T(8,128)S(1)} %get-tuple-element.208, f32[4,12,288,288]{2,3,1,0:T(8,128)} %get-tuple-element.200, f32[4,12,288]{2,1,0:T(8,128)S(1)} %get-tuple-element.199), kind=kLoop, calls=%fused_computation.1 | loop fusion | flops 15925248 | bytes 39923712 | tf_op jit(solution)/shard_map/convert_element_type | solution.py:149
  325.8 4.0 copy-done.2
  329.8 3.6 convert_reduce_fusion.2
  333.5 9.4 %fusion.31 = bf16[4,288,12,64]{1,3,2,0:T(8,128)(2,1)} fusion(bf16[4,12,288,288]{2,3,1,0:T(8,128)(2,1)} %copy-done.2, bf16[4,288,12,64]{1,0,3,2:T(4,128)(2,1)S(1)} %copy-done.4), kind=kOutput, calls=%fused_computation.73 | convolution fusion | flops 511377408 | bytes 11501568 | tf_op jit(solution)/shard_map/rhqk,rqhc->rkhc/dot_general | solution.py:153
  342.8 3.2 copy.198
  346.1 5.0 reshape.189
  351.1 3.2 copy.195
  354.3 4.8 reshape.188
  359.2 3.2 copy.192
  362.4 4.8 reshape.187
  367.2 3.3 fusion.48
  374.0 2.0 pad_maximum_fusion
  376.0 8.2 %copy.228 = bf16[3,768,768]{2,0,1:T(4,128)(2,1)} copy(bf16[3,768,768]{1,2,0:T(8,128)(2,1)} %pad_maximum_fusion) | data formatting | bytes 7077888
  384.1 4.9 copy.237
  389.7 12.2 %convolution_convert_fusion.1 = bf16[768,3072]{1,0:T(8,128)(2,1)} fusion(bf16[1152,3072]{1,0:T(8,128)(2,1)} %get-tuple-element.215, f32[1152,768]{1,0:T(8,128)} %copy-done.9, f32[768]{0:T(1024)S(1)} %copy-done.44, f32[1152]{0:T(1024)S(1)} %copy-done.24, f32[1152]{0:T(1024)S(1)} %broadcast_multiply_fusion.4, f32[768]{0:T(1024)S(1)} %copy-done.29), kind=kOutput, calls=%fused_computation.27 | convolution fusion | flops 5442600960 | bytes 15350784 | tf_op jit(solution)/shard_map/dot_general | solution.py:50
  402.1 1.7 copy.230
  405.5 11.2 %convolution_convert_fusion = bf16[768,3072]{1,0:T(8,128)(2,1)} fusion(bf16[1152,3072]{1,0:T(8,128)(2,1)} %get-tuple-element.203, f32[1152,768]{1,0:T(8,128)} %copy-done.13), kind=kOutput, calls=%fused_computation.26 | convolution fusion | flops 5439062016 | bytes 15335424 | tf_op jit(solution)/shard_map/dot_general | solution.py:50
  416.8 18.8 %reduce-scatter.25.cloned.1.call-done = bf16[96,2304]{1,0:T(8,128)(2,1)} async-done(((bf16[768,2304]{1,0:T(8,128)(2,1)}), bf16[96,2304]{1,0:T(8,128)(2,1)}) %reduce-scatter.25.cloned.1.call-update) | async-done | bytes 442384
  438.8 1.8 copy.202
  443.6 6.7 convolution_add_fusion.5
  450.3 43.0 %reduce-scatter.17.cloned.1.call-done = bf16[96,3072]{1,0:T(8,128)(2,1)} async-done(((bf16[768,3072]{1,0:T(8,128)(2,1)}), bf16[96,3072]{1,0:T(8,128)(2,1)}) %reduce-scatter.17.cloned.1.call-update) | async-done | bytes 589840 | tf_op jit(solution)/shard_map/reduce_scatter | solution.py:132
  493.6 4.5 convolution_add_fusion.4
  498.2 4.7 convolution_add_fusion.3
  503.0 12.6 %reduce-scatter.27.cloned.1.call-done = bf16[192,96]{1,0:T(8,128)(2,1)} async-done(((bf16[768,96]{1,0:T(8,128)(2,1)}), bf16[192,96]{1,0:T(8,128)(2,1)}) %reduce-scatter.27.cloned.1.call-update) | async-done | bytes 36880
  519.5 53.2 %all-gather.17.cloned.1.call-done = f32[32,12,768]{2,1,0:T(8,128)} async-done(((f32[1,12,768]{2,1,0:T(8,128)}), f32[32,12,768]{2,1,0:T(8,128)}) %all-gather.17.cloned.1.call-update) | async-done | bytes 1179664 | tf_op jit(solution)/shard_map/all_gather | solution.py:178
  574.6 54.6 %reduce-scatter.21.cloned.1.call-done = bf16[96,3072]{1,0:T(8,128)(2,1)} async-done(((bf16[768,3072]{1,0:T(8,128)(2,1)}), bf16[96,3072]{1,0:T(8,128)(2,1)}) %reduce-scatter.21.cloned.1.call-update) | async-done | bytes 589840 | tf_op jit(solution)/shard_map/reduce_scatter | solution.py:132
  633.0 20.5 %reduce-scatter.13.cloned.1.call-done = bf16[3,96,192]{1,2,0:T(8,128)(2,1)} async-done(((bf16[3,96,768]{1,2,0:T(8,128)(2,1)}), bf16[3,96,192]{1,2,0:T(8,128)(2,1)}) %reduce-scatter.13.cloned.1.call-update) | async-done | bytes 110608 | tf_op jit(solution)/shard_map/reduce_scatter | solution.py:133
  658.2 17.9 %reduce-scatter.19.cloned.1.call-done = bf16[96,768]{1,0:T(8,128)(2,1)} async-done(((bf16[96,3072]{1,0:T(8,128)(2,1)}), bf16[96,768]{1,0:T(8,128)(2,1)}) %reduce-scatter.19.cloned.1.call-update) | async-done | bytes 147472 | tf_op jit(solution)/shard_map/reduce_scatter | solution.py:133
  676.1 2.3 fusion.76
  678.4 20.3 %reduce-scatter.23.cloned.1.call-done = bf16[96,768]{1,0:T(8,128)(2,1)} async-done(((bf16[96,3072]{1,0:T(8,128)(2,1)}), bf16[96,768]{1,0:T(8,128)(2,1)}) %reduce-scatter.23.cloned.1.call-update) | async-done | bytes 147472 | tf_op jit(solution)/shard_map/reduce_scatter | solution.py:133
  698.7 2.4 fusion.72
  (210 shorter events, 37.9 us)
Async XLA Ops:
  7.2 40.9 %copy-start = (bf16[768,768]{1,0:T(8,128)(2,1)S(1)}, bf16[768,768]{1,0:T(8,128)(2,1)}, u32[]{:S(2)}) copy-start(bf16[768,768]{1,0:T(8,128)(2,1)} %param.37) | copy-start | bytes 3538948
  7.2 103.6 %all-gather.9.cloned.1.call-start = ((), (), s32[]{:S(2)}) async-start(), calls=%async_computation.8 | async-start | bytes 3981312 | tf_op jit(solution)/shard_map/all_gather | solution.py:69
  8.6 74.2 %copy-start.48 = (bf16[2,3,64]{2,0,1:T(2,128)(2,1)S(1)}, bf16[2,3,64]{2,0,1:T(2,128)(2,1)}, u32[]{:S(2)}) copy-start(bf16[2,3,64]{2,0,1:T(2,128)(2,1)} %param.35) | copy-start | bytes 2308
  30.3 65.6 %copy-start.32 = (bf16[6,768]{1,0:T(8,128)(2,1)S(1)}, bf16[6,768]{1,0:T(8,128)(2,1)}, u32[]{:S(2)}) copy-start(bf16[6,768]{1,0:T(8,128)(2,1)} %param.40) | copy-start | bytes 27652
  30.3 65.7 %copy-start.34 = (bf16[12,64]{1,0:T(8,128)(2,1)S(1)}, bf16[12,64]{1,0:T(8,128)(2,1)}, u32[]{:S(2)}) copy-start(bf16[12,64]{1,0:T(8,128)(2,1)} %param.38) | copy-start | bytes 4612
  30.3 78.9 %copy-start.6 = (bf16[4,288,768]{2,1,0:T(8,128)(2,1)S(1)}, bf16[4,288,768]{2,1,0:T(8,128)(2,1)}, u32[]{:S(2)}) copy-start(bf16[4,288,768]{2,1,0:T(8,128)(2,1)} %param.32) | copy-start | bytes 5308420
  32.6 161.5 %all-gather.11.cloned.1.call-start = ((), (), s32[]{:S(2)}) async-start(), calls=%async_computation.9 | async-start | bytes 1327104 | tf_op jit(solution)/shard_map/all_gather | solution.py:73
  48.0 152.6 %all-gather.13.cloned.1.call-start = ((), (), s32[]{:S(2)}) async-start(), calls=%async_computation.10 | async-start | bytes 5308416 | tf_op jit(solution)/shard_map/all_gather | solution.py:77
  65.6 148.8 %all-gather.15.cloned.1.call-start = ((), (), s32[]{:S(2)}) async-start(), calls=%async_computation.11 | async-start | bytes 5308416 | tf_op jit(solution)/shard_map/all_gather | solution.py:81
  82.7 319.3 %reduce-scatter.15.cloned.1.call-start = ((), (), s32[]{:S(2)}) async-start(), calls=%async_computation.13 | async-start | bytes 1327104 | tf_op jit(solution)/shard_map/reduce_scatter | solution.py:132
  95.9 118.5 %copy-start.43 = (f32[768]{0:T(1024)}, f32[768]{0:T(1024)S(1)}, u32[]{:S(2)}) copy-start(f32[768]{0:T(1024)S(1)} %get-tuple-element.161) | copy-start | bytes 9220
  96.0 163.1 %copy-start.28 = (f32[768]{0:T(1024)}, f32[768]{0:T(1024)S(1)}, u32[]{:S(2)}) copy-start(f32[768]{0:T(1024)S(1)} %get-tuple-element.163) | copy-start | bytes 9220
  120.5 21.9 %copy-start.3 = (bf16[4,288,12,64]{1,0,3,2:T(4,128)(2,1)}, bf16[4,288,12,64]{1,0,3,2:T(4,128)(2,1)S(1)}, u32[]{:S(2)}) copy-start(bf16[4,288,12,64]{1,0,3,2:T(4,128)(2,1)S(1)} %reshape.182) | copy-start | bytes 5308420
  154.3 25.9 %copy-start.15 = (bf16[4,288,12,64]{1,0,3,2:T(4,128)(2,1)S(1)}, bf16[4,288,12,64]{1,0,3,2:T(4,128)(2,1)}, u32[]{:S(2)}) copy-start(bf16[4,288,12,64]{1,0,3,2:T(4,128)(2,1)} %reshape.181) | copy-start | bytes 5308420
  198.2 1.8 copy-start.9
  200.6 58.5 %copy-start.23 = (f32[1152]{0:T(1024)}, f32[1152]{0:T(1024)S(1)}, u32[]{:S(2)}) copy-start(f32[1152]{0:T(1024)S(1)} %add_rsqrt_fusion.1) | copy-start | bytes 13828
  226.2 1.5 copy-start.7
  229.6 3.1 copy-start.49
  229.6 19.7 %slice-start = ((s8[4718592]{0:T(1024)(128)(4,1)}), s8[4194304]{0:T(1024)(128)(4,1)S(1)}, s32[]{:S(2)}) async-start(s8[4718592]{0:T(1024)(128)(4,1)} %bitcast.135), calls=%async_computation.21 | async-start | bytes 8388608
  232.7 16.6 %copy-start.13 = (f32[1152,768]{1,0:T(8,128)}, f32[1152,768]{1,0:T(8,128)S(1)}, u32[]{:S(2)}) copy-start(f32[1152,768]{1,0:T(8,128)S(1)} %get-tuple-element.184) | copy-start | bytes 10616836
  232.7 16.6 %copy-start.10 = (f32[1152,768]{1,0:T(8,128)S(1)}, f32[1152,768]{1,0:T(8,128)}, u32[]{:S(2)}) copy-start(f32[1152,768]{1,0:T(8,128)} %copy-done.9) | copy-start | bytes 10616836
  232.7 16.6 %slice-start.1 = ((s8[4718592]{0:T(1024)(128)(4,1)}), s8[524288]{0:T(1024)(128)(4,1)S(1)}, s32[]{:S(2)}) async-start(s8[4718592]{0:T(1024)(128)(4,1)} %bitcast.135), calls=%async_computation.22 | async-start | bytes 1048576
  259.1 3.6 copy-start.51
  260.9 1.8 copy-start.12
  311.2 18.6 %copy-start.5 = (bf16[4,288,12,64]{1,0,3,2:T(4,128)(2,1)S(1)}, bf16[4,288,12,64]{1,0,3,2:T(4,128)(2,1)}, u32[]{:S(2)}) copy-start(bf16[4,288,12,64]{1,0,3,2:T(4,128)(2,1)} %reshape.183) | copy-start | bytes 5308420
  325.8 4.0 copy-start.2
  329.8 3.7 copy-start.4
  333.4 102.2 %reduce-scatter.25.cloned.1.call-start = ((), (), s32[]{:S(2)}) async-start(), calls=%async_computation.19 | async-start | bytes 3981312
  333.5 9.4 %copy-start.14 = (bf16[4,288,12,64]{1,3,2,0:T(8,128)(2,1)S(1)}, bf16[4,288,12,64]{1,3,2,0:T(8,128)(2,1)}, u32[]{:S(2)}) copy-start(bf16[4,288,12,64]{1,3,2,0:T(8,128)(2,1)} %get-tuple-element.213) | copy-start | bytes 5308420
  342.8 8.3 %copy-start.8 = (bf16[4,288,12,64]{1,3,2,0:T(8,128)(2,1)S(1)}, bf16[4,288,12,64]{1,3,2,0:T(8,128)(2,1)}, u32[]{:S(2)}) copy-start(bf16[4,288,12,64]{1,3,2,0:T(8,128)(2,1)} %fusion.31) | copy-start | bytes 5308420
  354.3 4.8 copy-start.11
  362.4 4.8 copy-start.16
  367.2 3.3 copy-start.17
  367.2 3.4 copy-start.50
  370.5 1.7 copy-start.18
  389.1 104.3 %reduce-scatter.17.cloned.1.call-start = ((), (), s32[]{:S(2)}) async-start(), calls=%async_computation.14 | async-start | bytes 5308416 | tf_op jit(solution)/shard_map/reduce_scatter | solution.py:132
  401.9 2.0 copy-start.25
  401.9 2.0 copy-start.33
  401.9 2.2 copy-start.27
  401.9 2.2 copy-start.42
  401.9 2.2 copy-start.41
  401.9 2.2 copy-start.31
  402.0 2.2 copy-start.26
  402.0 2.2 copy-start.30
  402.0 113.6 %reduce-scatter.27.cloned.1.call-start = ((), (), s32[]{:S(2)}) async-start(), calls=%async_computation.20 | async-start | bytes 245760
  403.8 168.9 %all-gather.17.cloned.1.call-start = ((), (), s32[]{:S(2)}) async-start(), calls=%async_computation.18 | async-start | bytes 1622016 | tf_op jit(solution)/shard_map/all_gather | solution.py:178
  405.5 223.7 %reduce-scatter.21.cloned.1.call-start = ((), (), s32[]{:S(2)}) async-start(), calls=%async_computation.16 | async-start | bytes 5308416 | tf_op jit(solution)/shard_map/reduce_scatter | solution.py:132
  416.7 21.8 %copy-start.20 = (f32[3,96,192]{2,1,0:T(8,128)S(1)}, f32[3,96,192]{2,1,0:T(8,128)}, u32[]{:S(2)}) copy-start(f32[3,96,192]{2,1,0:T(8,128)} %param.42) | copy-start | bytes 663556
  416.7 21.9 %copy-start.21 = (f32[3,96,192]{2,1,0:T(8,128)S(1)}, f32[3,96,192]{2,1,0:T(8,128)}, u32[]{:S(2)}) copy-start(f32[3,96,192]{2,1,0:T(8,128)} %param.43) | copy-start | bytes 663556
  416.7 236.8 %reduce-scatter.13.cloned.1.call-start = ((), (), s32[]{:S(2)}) async-start(), calls=%async_computation.12 | async-start | bytes 737280 | tf_op jit(solution)/shard_map/reduce_scatter | solution.py:133
  438.4 237.6 %reduce-scatter.19.cloned.1.call-start = ((), (), s32[]{:S(2)}) async-start(), calls=%async_computation.15 | async-start | bytes 737280 | tf_op jit(solution)/shard_map/reduce_scatter | solution.py:133
  493.4 205.3 %reduce-scatter.23.cloned.1.call-start = ((), (), s32[]{:S(2)}) async-start(), calls=%async_computation.17 | async-start | bytes 737280 | tf_op jit(solution)/shard_map/reduce_scatter | solution.py:133
  502.9 126.4 %copy-start.45 = (f32[2,3,8]{2,0,1:T(2,128)S(1)}, f32[2,3,8]{2,0,1:T(2,128)}, u32[]{:S(2)}) copy-start(f32[2,3,8]{2,0,1:T(2,128)} %param.45) | copy-start | bytes 580
  502.9 126.4 %copy-start.46 = (f32[2,3,8]{2,0,1:T(2,128)S(1)}, f32[2,3,8]{2,0,1:T(2,128)}, u32[]{:S(2)}) copy-start(f32[2,3,8]{2,0,1:T(2,128)} %param.44) | copy-start | bytes 580
  502.9 126.4 %copy-start.47 = (f32[2,3,8]{2,0,1:T(2,128)S(1)}, f32[2,3,8]{2,0,1:T(2,128)}, u32[]{:S(2)}) copy-start(f32[2,3,8]{2,0,1:T(2,128)} %param.46) | copy-start | bytes 580
  502.9 128.8 %copy-start.35 = (f32[6,24]{1,0:T(8,128)S(1)}, f32[6,24]{1,0:T(8,128)}, u32[]{:S(2)}) copy-start(f32[6,24]{1,0:T(8,128)} %param.59) | copy-start | bytes 1732
  502.9 128.8 %copy-start.36 = (f32[6,24]{1,0:T(8,128)S(1)}, f32[6,24]{1,0:T(8,128)}, u32[]{:S(2)}) copy-start(f32[6,24]{1,0:T(8,128)} %param.60) | copy-start | bytes 1732
  502.9 128.8 %copy-start.37 = (f32[6,24]{1,0:T(8,128)S(1)}, f32[6,24]{1,0:T(8,128)}, u32[]{:S(2)}) copy-start(f32[6,24]{1,0:T(8,128)} %param.61) | copy-start | bytes 1732
  502.9 129.5 %copy-start.38 = (f32[12,8]{0,1:T(8,128)S(1)}, f32[12,8]{0,1:T(8,128)}, u32[]{:S(2)}) copy-start(f32[12,8]{0,1:T(8,128)} %param.53) | copy-start | bytes 1156
  502.9 129.5 %copy-start.39 = (f32[12,8]{0,1:T(8,128)S(1)}, f32[12,8]{0,1:T(8,128)}, u32[]{:S(2)}) copy-start(f32[12,8]{0,1:T(8,128)} %param.54) | copy-start | bytes 1156
  502.9 129.5 %copy-start.40 = (f32[12,8]{0,1:T(8,128)S(1)}, f32[12,8]{0,1:T(8,128)}, u32[]{:S(2)}) copy-start(f32[12,8]{0,1:T(8,128)} %param.55) | copy-start | bytes 1156
  502.9 150.6 %copy-start.19 = (f32[3,96,192]{1,2,0:T(8,128)S(1)}, f32[3,96,192]{1,2,0:T(8,128)}, u32[]{:S(2)}) copy-start(f32[3,96,192]{1,2,0:T(8,128)} %copy.202) | copy-start | bytes 663556
  517.3 158.7 %copy-start.22 = (f32[96,768]{1,0:T(8,128)S(1)}, f32[96,768]{1,0:T(8,128)}, u32[]{:S(2)}) copy-start(f32[96,768]{1,0:T(8,128)} %param.50) | copy-start | bytes 884740
  653.5 47.6 %copy-start.1 = (bf16[768,768]{1,0:T(8,128)(2,1)S(1)}, bf16[768,768]{1,0:T(8,128)(2,1)}, u32[]{:S(2)}) copy-start(bf16[768,768]{1,0:T(8,128)(2,1)} %param.37) | copy-start | bytes 3538948
  (3 other events, 2.1 us)
Sparse Core Ops, SparseCore 0:
  32.7 33.7 all-gather.8
  68.9 24.0 all-gather.10
  94.9 38.9 all-gather.12
  135.6 38.9 all-gather.14
  333.5 35.0 reduce-scatter.14
  389.2 46.3 reduce-scatter.24
  439.4 53.8 reduce-scatter.16
  496.2 19.3 reduce-scatter.26
  519.5 53.2 all-gather.16
  576.4 52.7 reduce-scatter.20
  631.5 21.9 reduce-scatter.12
  655.7 20.3 reduce-scatter.18
  678.3 20.3 reduce-scatter.22
